TPU v7x, 128 devices: a whole 4x4x4 slice. The times are simulated.
128 devices in a mesh: walk: 16 (over x, z), pan: 8 (over y, core).
Axes of the slice: x: 4, y: 4, z: 4, core: 2. Of those that a mesh axis runs over, the one named last changes fastest.
Arguments:
- dlog: bfloat16 [32768, 4096], P('walk', 'pan'), may hold values from 0 to 2
- dener: bfloat16 [32768, 4096], P('walk', 'pan'), may hold values from -0.5 to 2.5
- energy: float32 [32768], P('walk'), may hold values from -3 to -1
- mask: int32 [16], replicated, may hold values 0 or 1
- owner: int32 [16], replicated, may hold values from 0 to 15, each once
Outputs:
- correlation: float32 [4096, 4096], P('walk', 'pan')
- hamilton: float32 [4096, 4096], P('walk', 'pan')
Inputs may be any that keep to these rules, and one draw needn't show every extreme that they name: `owner`: each block number appears once.
All inputs are finite; a program needn't handle non-finite values.
Results may differ from a plain program's by a relative error of at most 0.005.
Values may be sent and summed in bfloat16 or wider, within the bound.
A program may use at most 128 MiB of HBM per device.

v0:
```python
import jax
import jax.numpy as jnp
from jax import lax
from jax.sharding import PartitionSpec as P

BLOCK = 256


def per_device(dlog, dener, energy, mask, owner):
    wdev, width = dlog.shape
    total = wdev * lax.axis_size("walk")
    full = width * lax.axis_size("pan")
    nblocks = full // BLOCK
    first = lax.axis_index("pan") * (width // BLOCK)
    local_mask = lax.dynamic_slice_in_dim(mask, first, width // BLOCK)
    colmask = jnp.repeat(local_mask, BLOCK).astype(jnp.float32)
    om = dlog.astype(jnp.float32) * colmask
    gm = dener.astype(jnp.float32) * colmask
    osum, gsum, esum = lax.psum((jnp.sum(om, 0), jnp.sum(gm, 0), jnp.sum(energy)), "walk")
    ocf = om - osum / total
    oc = ocf.astype(jnp.bfloat16)
    hc = ((energy - esum / total)[:, None] * ocf + gm - gsum / total).astype(jnp.bfloat16)
    gathered = lax.all_gather(oc, "pan", axis=1, tiled=True)
    ordered = jnp.take(gathered.reshape(wdev, nblocks, BLOCK), owner, axis=1).reshape(wdev, full)
    right_side = jnp.concatenate([oc, hc], 1)
    dims = (((0,), (0,)), ((), ()))
    terms = lax.dot_general(ordered, right_side, dims, preferred_element_type=jnp.float32)
    shares = lax.psum_scatter(terms, "walk", scatter_dimension=0, tiled=True)
    shares = shares / total
    return (shares[:, :width], shares[:, width:])


def solution(mesh):
    return jax.shard_map(
        per_device,
        mesh=mesh,
        in_specs=(P("walk", "pan"), P("walk", "pan"), P("walk"), P(), P()),
        out_specs=(P("walk", "pan"), P("walk", "pan")),
        check_vma=False,
    )
```

profile of v0, /device:TPU:1, one launch (start us, length us, event | category | flops | bytes accessed | tf_op | source)
XLA Modules:
  0.0 329.0 jit_solution(5466082891426086491)
XLA Ops:
  7.2 0.0 copy-start.3
  7.2 0.0 copy-start
  7.2 0.0 all-gather.2.cloned.1.call-start
  7.2 0.9 dynamic-slice_convert_fusion
  8.1 0.1 broadcast_bitcast_fusion
  8.2 1.3 reduce_sum.28
  9.5 3.1 fusion.4
  12.6 36.5 %all-reduce = (f32[512]{0:T(512)S(1)}, f32[512]{0:T(512)S(1)}, f32[]{:T(128)}) all-reduce(f32[512]{0:T(512)S(1)} %get-tuple-element.3, f32[512]{0:T(512)S(1)} %get-tuple-element.2, f32[]{:T(128)} %reduce_sum.28), channel_id=1, replica_groups=mesh['walk'=16,'pan'=8] {'walk'}, use_global_device_ids=true, to_apply=%region_1.0 | all-reduce | flops 1025 | bytes 8200 | tf_op jit(solution)/shard_map/psum | solution.py:19
  49.7 0.0 copy-done.3
  49.7 0.0 copy-done
  49.7 0.0 copy-start.4
  49.8 3.9 %subtract_convert_fusion = (bf16[2048,512]{1,0:T(8,128)(2,1)}, bf16[2048,512]{1,0:T(8,128)(2,1)}) fusion(bf16[2048,512]{1,0:T(8,128)(2,1)S(1)} %copy-done, bf16[2048,512]{1,0:T(8,128)(2,1)} %param.5, f32[512]{0:T(512)S(1)} %get-tuple-element.11, f32[2048]{0:T(1024)S(1)} %broadcast_subtract_fusion, f32[512]{0:T(512)S(1)} %get-tuple-element.12, f32[512]{0:T(512)S(1)} %bitcast.11), kind=kLoop, calls=%fused_computation.6 | loop fusion | flops 10485760 | bytes 8402944 | tf_op jit(solution)/shard_map/convert_element_type | solution.py:22
  53.6 0.0 all-gather.2.cloned.1.call-update
  53.7 0.0 reduce-scatter.2.cloned.1.call-start
  53.7 0.0 copy-done.4
  53.7 0.1 broadcast_in_dim.24
  53.9 89.0 %all-gather.2.cloned.1.call-done = bf16[2048,4096]{1,0:T(8,128)(2,1)} async-done(((bf16[2048,512]{1,0:T(8,128)(2,1)}), bf16[2048,4096]{1,0:T(8,128)(2,1)}) %all-gather.2.cloned.1.call-update) | async-done | bytes 16777232 | tf_op jit(solution)/shard_map/all_gather | solution.py:23
  142.8 22.6 %copy.7 = bf16[2048,4096]{0,1:T(8,128)(2,1)} copy(bf16[2048,4096]{1,0:T(8,128)(2,1)} %all-gather.2.cloned.1.call-done) | data formatting | bytes 33554432 | tf_op jit(solution)/shard_map/all_gather | solution.py:23
  165.4 13.0 %gather_fusion = bf16[16,2048,256]{1,2,0:T(8,128)(2,1)} fusion(bf16[2048,16,256]{0,2,1:T(8,128)(2,1)} %bitcast.9, s32[1024]{0:T(1024)S(1)} %pad_clamp_fusion), kind=kCustom, calls=%fused_computation | custom fusion | bytes 33554496 | tf_op jit(solution)/shard_map/jit(_take)/gather | solution.py:24
  178.4 0.0 copy-start.1
  178.4 0.0 copy-start.2
  178.4 9.5 %bitcast_select_fusion = bf16[2048,4096]{0,1:T(8,128)(2,1)S(1)} fusion(bf16[16,2048,256]{1,2,0:T(8,128)(2,1)} %gather_fusion, pred[4096]{0:T(1024)(128)(4,1)S(1)} %broadcast_in_dim.25), kind=kLoop, calls=%fused_computation.1 | loop fusion | flops 8388608 | bytes 33558528 | tf_op jit(solution)/shard_map/jit(_take)/select_n | solution.py:24
  188.0 0.0 copy-done.1
  188.0 0.0 copy-done.2
  188.0 20.8 %fusion = f32[4096,1024]{1,0:T(8,128)} fusion(bf16[2048,4096]{0,1:T(8,128)(2,1)S(1)} %bitcast_select_fusion, bf16[2048,512]{1,0:T(8,128)(2,1)S(1)} %copy-done.2, bf16[2048,512]{1,0:T(8,128)(2,1)S(1)} %copy-done.1), kind=kOutput, calls=%fused_computation.2 | convolution fusion | flops 17188257792 | bytes 37748736 | tf_op jit(solution)/shard_map/dot_general | solution.py:27
  208.8 0.0 reduce-scatter.2.cloned.1.call-update
  208.8 111.0 %reduce-scatter.2.cloned.1.call-done = f32[256,1024]{1,0:T(8,128)} async-done(((f32[4096,1024]{1,0:T(8,128)}), f32[256,1024]{1,0:T(8,128)}) %reduce-scatter.2.cloned.1.call-update) | async-done | bytes 1048592 | tf_op jit(solution)/shard_map/reduce_scatter | solution.py:28
  319.8 1.3 broadcast_multiply_fusion
  321.1 1.0 fusion.9
  (7 shorter events, 0.0 us)
Async XLA Ops:
  7.2 42.5 %copy-start.3 = (f32[2048]{0:T(1024)S(1)}, f32[2048]{0:T(1024)}, u32[]{:S(2)}) copy-start(f32[2048]{0:T(1024)} %param.7) | copy-start | bytes 24580
  7.2 42.6 %copy-start = (bf16[2048,512]{1,0:T(8,128)(2,1)S(1)}, bf16[2048,512]{1,0:T(8,128)(2,1)}, u32[]{:S(2)}) copy-start(bf16[2048,512]{1,0:T(8,128)(2,1)} %param.6) | copy-start | bytes 6291460
  7.2 135.6 %all-gather.2.cloned.1.call-start = ((), (), s32[]{:S(2)}) async-start(), calls=%async_computation.1 | async-start | bytes 18874368 | tf_op jit(solution)/shard_map/all_gather | solution.py:23
  49.7 4.0 %copy-start.4 = (s32[16]{0:T(128)S(1)}, s32[16]{0:T(128)}, u32[]{:S(2)}) copy-start(s32[16]{0:T(128)} %param.9) | copy-start | bytes 196
  53.7 266.1 %reduce-scatter.2.cloned.1.call-start = ((), (), s32[]{:S(2)}) async-start(), calls=%async_computation.2 | async-start | bytes 17825792 | tf_op jit(solution)/shard_map/reduce_scatter | solution.py:28
  178.4 9.6 %copy-start.1 = (bf16[2048,512]{1,0:T(8,128)(2,1)S(1)}, bf16[2048,512]{1,0:T(8,128)(2,1)}, u32[]{:S(2)}) copy-start(bf16[2048,512]{1,0:T(8,128)(2,1)} %get-tuple-element.8) | copy-start | bytes 6291460
  178.4 9.6 %copy-start.2 = (bf16[2048,512]{1,0:T(8,128)(2,1)S(1)}, bf16[2048,512]{1,0:T(8,128)(2,1)}, u32[]{:S(2)}) copy-start(bf16[2048,512]{1,0:T(8,128)(2,1)} %get-tuple-element.7) | copy-start | bytes 6291460
Sparse Core Ops, SparseCore 0:
  53.8 88.9 all-gather.1
  209.0 110.7 reduce-scatter.1
where the time goes:
time: 330 us; the launch traced here: 329 us
  waiting for transfers between devices  200 us (61%)
  local copies, waits for them, and re-layouts  36.8 us (11%)
  blocking collectives  36.5 us (11%)
  matrix products  20.8 us (6%)
  other arithmetic  20.1 us (6%)
  between operations  14.8 us (4%)
    reduce_scatter x1, waiting for transfers between devices, per_device(): shares = lax.psum_scatter(terms, 'walk', scatter_dimension=0, tiled=True)  111 us
    all_gather x1, waiting for transfers between devices, per_device(): gathered = lax.all_gather(oc, 'pan', axis=1, tiled=True)  89 us
    psum x1, blocking collectives, per_device(): lax.psum((jnp.sum(om, 0), jnp.sum(gm, 0), jnp.sum(energy)), 'walk')  36.5 us
    all_gather x1, local copies, waits for them, and re-layouts, per_device(): gathered = lax.all_gather(oc, 'pan', axis=1, tiled=True)  22.6 us
    dot_general x1, matrix products, per_device(): lax.dot_general(ordered, right_side, dims, preferred_element_type=jnp.flo...  20.8 us
    gather x1, local copies, waits for them, and re-layouts, per_device(): jnp.take(gathered.reshape(wdev, nblocks, BLOCK), owner, axis=1)  13 us
    select_n x2, other arithmetic, per_device(): jnp.take(gathered.reshape(wdev, nblocks, BLOCK), owner, axis=1)  9.55 us
  transfers between devices with their start and end apart: 2, of which 2 were waited for; matrix products, arithmetic and copies ran while one was open for 0% of the time, Pallas kernels for 0%

commit v1 on v0

v1 whole, which is shorter than its diff:
```python
import jax
import jax.numpy as jnp
from jax import lax
from jax.experimental import pallas as pl
from jax.experimental.pallas import tpu as pltpu
from jax.sharding import PartitionSpec as P

BLOCK = 256
ROUNDS = 4
MESH = pl.DeviceIdType.MESH
F32 = jnp.float32
BF16 = jnp.bfloat16


def wrap4(v):
    return lax.rem(v, 4)


def kernel(
    mask, owner, dlog, dener, energy, out_c, out_h,
    blocks, gown, opar, gpar, right, left_t, spread,
    part, ring1, half, ring2, whole, give, staged, stats, means, pmeans,
    local_sem, ag_send, ag_recv, pt_send, pt_recv, st_send, st_recv, mm_send, mm_recv,
    r1_send, r1_recv, r2_send, r2_recv, z_send, z_recv, f_send, f_recv,
):
    walkers = dlog.shape[0]
    total = walkers * 16
    scale = 1.0 / total
    chunk = 256
    steps = walkers // chunk

    walk = lax.axis_index("walk")
    pan = lax.axis_index("pan")
    px, pz = lax.div(walk, 4), lax.rem(walk, 4)
    py, core = lax.div(pan, 2), lax.rem(pan, 2)
    partner = (walk, py * 2 + (1 - core))

    def at_y(shift):
        return (walk, wrap4(py + shift) * 2 + core)

    def remote(src, dst, send, recv, device):
        return pltpu.make_async_remote_copy(
            src_ref=src, dst_ref=dst, send_sem=send, recv_sem=recv, device_id=device, device_id_type=MESH
        )

    own = [
        pltpu.make_async_copy(dlog.at[:, pl.ds(b * BLOCK, BLOCK)], blocks.at[b], local_sem.at[b]) for b in range(2)
    ] + [pltpu.make_async_copy(dener, gown, local_sem.at[2])]
    for copy in own:
        copy.start()

    barrier = pltpu.get_barrier_semaphore()

    def greet(d, carry):
        pl.semaphore_signal(barrier, inc=1, device_id=(lax.rem(walk + d, 16), pan), device_id_type=MESH)
        return carry

    lax.fori_loop(1, 16, greet, 0)
    for d in range(1, 4):
        pl.semaphore_signal(barrier, inc=1, device_id=at_y(d), device_id_type=MESH)
    pl.semaphore_signal(barrier, inc=1, device_id=partner, device_id_type=MESH)
    pl.semaphore_wait(barrier, 19)

    def column(b):
        return dlog.at[:, pl.ds(b * BLOCK, BLOCK)]

    gather = [
        remote(column(0), blocks.at[2], ag_send.at[0], ag_recv.at[0], at_y(1)),
        remote(column(1), blocks.at[3], ag_send.at[1], ag_recv.at[1], at_y(3)),
        remote(column(1), blocks.at[4], ag_send.at[2], ag_recv.at[2], at_y(1)),
        remote(column(0), blocks.at[5], ag_send.at[3], ag_recv.at[3], at_y(3)),
        remote(blocks.at[2], blocks.at[6], ag_send.at[4], ag_recv.at[4], at_y(1)),
        remote(blocks.at[3], blocks.at[7], ag_send.at[5], ag_recv.at[5], at_y(3)),
    ]
    for copy in gather[:4]:
        copy.start()
    pair = [
        remote(dlog, opar, pt_send.at[0], pt_recv.at[0], partner),
        remote(dener, gpar, pt_send.at[1], pt_recv.at[1], partner),
    ]
    for copy in pair:
        copy.start()

    for copy in own:
        copy.wait()
    esum = jnp.sum(energy[...])
    for b in range(2):

        def add(i, carry):
            rows = pl.ds(pl.multiple_of(i * chunk, chunk), chunk)
            o = jnp.sum(blocks[b, rows, :].astype(F32), axis=0, keepdims=True)
            g = jnp.sum(gown[rows, b * BLOCK:(b + 1) * BLOCK].astype(F32), axis=0, keepdims=True)
            return carry[0] + o, carry[1] + g

        zero = jnp.zeros((1, BLOCK), F32)
        o, g = lax.fori_loop(0, steps, add, (zero, zero))
        stats[walk, b] = jnp.concatenate([o, g, jnp.full((1, BLOCK), esum, F32), jnp.zeros((5, BLOCK), F32)], axis=0)

    def stat_copy(d):
        return remote(
            stats.at[walk], stats.at[walk], st_send.at[d], st_recv.at[d], (lax.rem(walk + d, 16), pan)
        )

    def stat_start(d, carry):
        stat_copy(d).start()
        return carry

    def stat_wait(d, carry):
        stat_copy(d).wait()
        return carry

    lax.fori_loop(1, 16, stat_start, 0)
    lax.fori_loop(1, 16, stat_wait, 0)
    sums = stats[0]
    for i in range(1, 16):
        sums = sums + stats[i]
    means[py] = sums * scale
    shared = [remote(means.at[py], means.at[py], mm_send.at[d], mm_recv.at[d], at_y(d)) for d in range(1, 4)] + [
        remote(means.at[py], pmeans, mm_send.at[0], mm_recv.at[0], partner)
    ]
    for copy in shared:
        copy.start()

    ebar = means[py, 0, 2:3, 0:128]
    for i in range(walkers // 128):
        row = energy[i:i + 1, :] - ebar
        spread[i * 128:(i + 1) * 128, :] = jnp.broadcast_to(row, (128, 128)).T

    def build(o_of, g_of, obar, gbar, m, tile):
        def step(i, carry):
            rows = pl.ds(pl.multiple_of(i * chunk, chunk), chunk)
            oc = o_of(rows).astype(F32) * m - obar
            e = spread[rows, :]
            hc = jnp.concatenate([e, e], axis=1) * oc + g_of(rows).astype(F32) * m - gbar
            right[0, tile, rows, :] = oc.astype(BF16)
            right[1, tile, rows, :] = hc.astype(BF16)
            return carry

        lax.fori_loop(0, steps, step, 0)

    for b in range(2):
        m = mask[py * 4 + core * 2 + b].astype(F32)
        build(
            lambda rows, b=b: blocks[b, rows, :],
            lambda rows, b=b: gown[rows, b * BLOCK:(b + 1) * BLOCK],
            means[py, b, 0:1, :] * m,
            means[py, b, 1:2, :] * m,
            m,
            core * 2 + b,
        )
    for copy in pair:
        copy.wait()
    for copy in shared:
        copy.wait()
    for b in range(2):
        m = mask[py * 4 + (1 - core) * 2 + b].astype(F32)
        build(
            lambda rows, b=b: opar[rows, b * BLOCK:(b + 1) * BLOCK],
            lambda rows, b=b: gpar[rows, b * BLOCK:(b + 1) * BLOCK],
            pmeans[b, 0:1, :] * m,
            pmeans[b, 1:2, :] * m,
            m,
            (1 - core) * 2 + b,
        )

    xs = (px, (wrap4(px + 1) * 4 + pz, pan), (wrap4(px + 3) * 4 + pz, pan))
    zs = (pz, (px * 4 + wrap4(pz + 1), pan), (px * 4 + wrap4(pz + 3), pan))

    def ring(buf, got, send, recv, axis):
        me, up, down = axis
        far, nxt, prv = wrap4(me + 2), wrap4(me + 1), wrap4(me + 3)
        return [
            remote(buf.at[0, far], got.at[0], send.at[0], recv.at[0], up),
            remote(buf.at[1, far], got.at[1], send.at[1], recv.at[1], down),
            remote(buf.at[1, nxt], got.at[2], send.at[2], recv.at[2], up),
            remote(buf.at[0, prv], got.at[3], send.at[3], recv.at[3], down),
            remote(buf.at[0, nxt], got.at[4], send.at[4], recv.at[4], up),
            remote(buf.at[1, prv], got.at[5], send.at[5], recv.at[5], down),
        ]

    def ring1_of(r, ch):
        return ring(part.at[r, ch], ring1.at[r, ch], r1_send.at[r, ch], r1_recv.at[r, ch], (xs, zs)[ch])

    def ring2_of(r, ch):
        return ring(half.at[r, ch], ring2.at[r, ch], r2_send.at[r, ch], r2_recv.at[r, ch], (zs, xs)[ch])

    def ring_start(copies):
        for copy in copies[:4]:
            copy.start()

    def ring_mid(copies, buf, got, axis):
        me = axis[0]
        for b, shift in ((0, 1), (1, 3)):
            copies[b].wait_recv()
            k = wrap4(me + shift)
            buf[b, k] = (buf[b, k].astype(F32) + got[b].astype(F32)).astype(BF16)
            copies[4 + b].start()

    def source(r, b):
        second = lax.div(r, 2) * (3 - r)
        middle = r - second - 3 * lax.div(r, 3)
        ysrc = wrap4(py + middle * (1 if b else 3) + 2 * lax.div(r, 3))
        bsel = b + second * (1 - 2 * b)
        return ysrc, bsel

    def block_of(r, b):
        ysrc, bsel = source(r, b)
        return ysrc * 4 + core * 2 + bsel

    def give_copy(r, b):
        return remote(give.at[r, b], whole.at[block_of(r, b)], z_send.at[r, b], z_recv.at[r, b], partner)

    def one_round(r, carry):
        for t in range(1, ROUNDS):

            @pl.when(r == t)
            def _():
                for b in range(2):
                    gather[2 * (t - 1) + b].wait_recv()
                    if t == 1:
                        gather[4 + b].start()

        for b in range(2):
            ysrc, bsel = source(r, b)
            m = mask[ysrc * 4 + core * 2 + bsel].astype(F32)
            obar = means[ysrc, bsel, 0:1, :] * m

            def turn(i, c):
                rows = pl.ds(pl.multiple_of(i * chunk, chunk), chunk)
                oc = blocks[2 * r + b, rows, :].astype(F32) * m - obar
                left_t[b * BLOCK:(b + 1) * BLOCK, rows] = oc.T.astype(BF16)
                return c

            lax.fori_loop(0, steps, turn, 0)

        for ch in range(2):
            for tile in range(4):
                product = jnp.dot(left_t[...], right[ch, tile], preferred_element_type=F32)
                h, off = tile // 2, (tile % 2) * BLOCK
                part[r, ch, :, :, h, :, off:off + BLOCK] = product.astype(BF16).reshape(2, 4, 64, BLOCK)
            ring_start(ring1_of(r, ch))

        for ch in range(2):
            ring_mid(ring1_of(r, ch), part.at[r, ch], ring1.at[r, ch], (xs, zs)[ch])
        for ch in range(2):
            copies = ring1_of(r, ch)
            me = (px, pz)[ch]
            for b, (i, j) in enumerate(((3, 4), (2, 5))):
                copies[i].wait_recv()
                copies[j].wait_recv()
                for k in range(4):
                    rows = slice(16 * k, 16 * k + 16)
                    value = (
                        part[r, ch, b, me, :, rows, :].astype(F32)
                        + ring1[r, ch, i, :, rows, :].astype(F32)
                        + ring1[r, ch, j, :, rows, :].astype(F32)
                    )
                    half[r, ch, b, k] = value.astype(BF16)
            ring_start(ring2_of(r, ch))
        for ch in range(2):
            ring_mid(ring2_of(r, ch), half.at[r, ch], ring2.at[r, ch], (zs, xs)[ch])
        for b, (i, j) in enumerate(((3, 4), (2, 5))):
            for ch in range(2):
                copies = ring2_of(r, ch)
                me = (pz, px)[ch]
                copies[i].wait_recv()
                copies[j].wait_recv()

                def value(h):
                    return (
                        half[r, ch, b, me, h].astype(F32)
                        + ring2[r, ch, i, h].astype(F32)
                        + ring2[r, ch, j, h].astype(F32)
                    ) * scale

                whole[block_of(r, b), ch] = value(core)
                give[r, b, ch] = value(1 - core)
            give_copy(r, b).start()
        return carry

    lax.fori_loop(0, ROUNDS, one_round, 0)

    def give_wait(r, carry):
        for b in range(2):
            give_copy(r, b).wait()
        return carry

    lax.fori_loop(0, ROUNDS, give_wait, 0)

    row_c = pl.multiple_of(px * 64 + pz * 16, 16)
    row_h = pl.multiple_of(pz * 64 + px * 16, 16)

    def place(r, d):
        return [
            remote(
                staged.at[r, ch],
                (out_c, out_h)[ch].at[pl.ds((row_c, row_h)[ch], 16), :],
                f_send.at[d, ch],
                f_recv.at[d, ch],
                (r, pan),
            )
            for ch in range(2)
        ]

    def place_start(d, carry):
        r = lax.rem(walk + d, 16)
        staged[r] = whole[owner[r]]
        for copy in place(r, d):
            copy.start()
        return carry

    def place_wait(d, carry):
        for copy in place(lax.rem(walk + d, 16), d):
            copy.wait()
        return carry

    lax.fori_loop(1, 16, place_start, 0)
    staged[walk] = whole[owner[walk]]
    mine = [
        pltpu.make_async_copy(
            staged.at[walk, ch], (out_c, out_h)[ch].at[pl.ds((row_c, row_h)[ch], 16), :], local_sem.at[ch]
        )
        for ch in range(2)
    ]
    for copy in mine:
        copy.start()
    for copy in gather:
        copy.wait_send()

    def sends(r, carry):
        for ch in range(2):
            for copy in ring1_of(r, ch) + ring2_of(r, ch):
                copy.wait_send()
        return carry

    lax.fori_loop(0, ROUNDS, sends, 0)
    for copy in mine:
        copy.wait()
    lax.fori_loop(1, 16, place_wait, 0)


def per_device(dlog, dener, energy, mask, owner):
    walkers, width = dlog.shape
    anywhere = pl.BlockSpec(memory_space=pl.ANY)
    scalars = pl.BlockSpec(memory_space=pltpu.SMEM)
    dma = pltpu.SemaphoreType.DMA
    out = jax.ShapeDtypeStruct((BLOCK, width), F32)
    return pl.pallas_call(
        kernel,
        out_shape=(out, out),
        in_specs=[scalars, scalars, anywhere, anywhere, pl.BlockSpec(memory_space=pltpu.VMEM)],
        out_specs=(anywhere, anywhere),
        scratch_shapes=[
            pltpu.VMEM((8, walkers, BLOCK), BF16),
            pltpu.VMEM((walkers, width), BF16),
            pltpu.VMEM((walkers, width), BF16),
            pltpu.VMEM((walkers, width), BF16),
            pltpu.VMEM((2, 4, walkers, BLOCK), BF16),
            pltpu.VMEM((2 * BLOCK, walkers), BF16),
            pltpu.VMEM((walkers, 128), F32),
            pltpu.VMEM((ROUNDS, 2, 2, 4, 2, 64, width), BF16),
            pltpu.VMEM((ROUNDS, 2, 6, 2, 64, width), BF16),
            pltpu.VMEM((ROUNDS, 2, 2, 4, 2, 16, width), BF16),
            pltpu.VMEM((ROUNDS, 2, 6, 2, 16, width), BF16),
            pltpu.VMEM((16, 2, 16, width), F32),
            pltpu.VMEM((ROUNDS, 2, 2, 16, width), F32),
            pltpu.VMEM((16, 2, 16, width), F32),
            pltpu.VMEM((16, 2, 8, BLOCK), F32),
            pltpu.VMEM((4, 2, 8, BLOCK), F32),
            pltpu.VMEM((2, 8, BLOCK), F32),
            dma((3,)), dma((6,)), dma((6,)), dma((2,)), dma((2,)), dma((16,)), dma((16,)), dma((4,)), dma((4,)),
            dma((ROUNDS, 2, 6)), dma((ROUNDS, 2, 6)), dma((ROUNDS, 2, 6)), dma((ROUNDS, 2, 6)),
            dma((ROUNDS, 2)), dma((ROUNDS, 2)), dma((16, 2)), dma((16, 2)),
        ],
        compiler_params=pltpu.CompilerParams(
            collective_id=0, has_side_effects=True, vmem_limit_bytes=64 * 1000 * 1000
        ),
    )(mask, owner, dlog, dener, energy.reshape(walkers // 128, 128))


def solution(mesh):
    return jax.shard_map(
        per_device,
        mesh=mesh,
        in_specs=(P("walk", "pan"), P("walk", "pan"), P("walk"), P(), P()),
        out_specs=(P("walk", "pan"), P("walk", "pan")),
        check_vma=False,
    )
```

time: 330 us -> 176 us (0.53)
  waiting for transfers between devices: 200 us -> 0 us
  Pallas kernels: 0 us -> 168 us
  blocking collectives: 36.5 us -> 0 us
  local copies, waits for them, and re-layouts: 36.8 us -> 3.74 us
  matrix products: 20.8 us -> 0 us
  other arithmetic: 20.1 us -> 0 us
  between operations: 14.8 us -> 0.64 us
    pallas_call x0 -> x1, Pallas kernels: none -> 168 us  [per_device(): pl.pallas_call(kernel, out_shape=(out, out), in_specs=[scalars, scalars,...]
    reduce_scatter x1 -> x0, waiting for transfers between devices: 111 us -> none  [per_device(): shares = lax.psum_scatter(terms, 'walk', scatter_dimension=0, tiled=True)]
    all_gather x1 -> x0, waiting for transfers between devices: 89 us -> none  [per_device(): gathered = lax.all_gather(oc, 'pan', axis=1, tiled=True)]
    psum x1 -> x0, blocking collectives: 36.5 us -> none  [per_device(): lax.psum((jnp.sum(om, 0), jnp.sum(gm, 0), jnp.sum(energy)), 'walk')]
    all_gather x1 -> x0, local copies, waits for them, and re-layouts: 22.6 us -> none  [per_device(): gathered = lax.all_gather(oc, 'pan', axis=1, tiled=True)]
    dot_general x1 -> x0, matrix products: 20.8 us -> none  [per_device(): lax.dot_general(ordered, right_side, dims, preferred_element_type=jnp.flo...]
    gather x1 -> x0, local copies, waits for them, and re-layouts: 13 us -> none  [per_device(): jnp.take(gathered.reshape(wdev, nblocks, BLOCK), owner, axis=1)]
    select_n x2 -> x0, other arithmetic: 9.55 us -> none  [per_device(): jnp.take(gathered.reshape(wdev, nblocks, BLOCK), owner, axis=1)]
  transfers between devices with their start and end apart: 2 -> 0, of which waited for: 2 -> 0; matrix products, arithmetic and copies ran while one was open for 0% -> 0% of each run, Pallas kernels for 0% -> 0%
where the time goes in v1:
time: 176 us; the launch traced here: 173 us
  Pallas kernels  168 us (95%)
  local copies, waits for them, and re-layouts  3.74 us (2%)
    pallas_call x1, Pallas kernels, per_device(): pl.pallas_call(kernel, out_shape=(out, out), in_specs=[scalars, scalars,...  168 us
    unnamed x2, local copies, waits for them, and re-layouts  3.74 us

profile of v1, /device:TPU:1, one launch (start us, length us, event | category | flops | bytes accessed | tf_op | source)
XLA Modules:
  0.0 172.5 jit_solution(17632011437040432381)
XLA Ops:
  0.6 168.1 %shard_map.68 = (f32[256,512]{1,0:T(8,128)}, f32[256,512]{1,0:T(8,128)}) custom-call(s32[16]{0:T(128)} %mask.1, s32[16]{0:T(128)} %owner.1, bf16[2048,512]{1,0:T(8,128)(2,1)} %dlog.1, bf16[2048,512]{1,0:T(8,128)(2,1)} %dener.1, f32[16,128]{1,0:T(8,128)} %bitcast.1), custom_call_target="tpu_custom_call" | custom-call | tf_op jit(solution)/shard_map/pallas_call | solution.py:348
  168.8 1.9 %copy.9 = f32[256,512]{1,0:T(8,128)} copy(f32[256,512]{1,0:T(8,128)} %get-tuple-element.4) | data formatting | bytes 1048576
  170.7 1.9 %copy.10 = f32[256,512]{1,0:T(8,128)} copy(f32[256,512]{1,0:T(8,128)} %get-tuple-element.5) | data formatting | bytes 1048576

commit v2 on v1

--- a/solution.py
+++ b/solution.py
@@ -17,7 +17,7 @@
 
 
 def kernel(
-    mask, owner, dlog, dener, energy, out_c, out_h,
+    mask, owner, dlog, dener, energy, out,
     blocks, gown, opar, gpar, right, left_t, spread,
     part, ring1, half, ring2, whole, give, staged, stats, means, pmeans,
     local_sem, ag_send, ag_recv, pt_send, pt_recv, st_send, st_recv, mm_send, mm_recv,
@@ -126,42 +126,47 @@
         row = energy[i:i + 1, :] - ebar
         spread[i * 128:(i + 1) * 128, :] = jnp.broadcast_to(row, (128, 128)).T
 
-    def build(o_of, g_of, obar, gbar, m, tile):
+    def build(o_of, g_of, obar, gbar, m, side, b):
         def step(i, carry):
             rows = pl.ds(pl.multiple_of(i * chunk, chunk), chunk)
             oc = o_of(rows).astype(F32) * m - obar
             e = spread[rows, :]
             hc = jnp.concatenate([e, e], axis=1) * oc + g_of(rows).astype(F32) * m - gbar
-            right[0, tile, rows, :] = oc.astype(BF16)
-            right[1, tile, rows, :] = hc.astype(BF16)
+            right[0, side, b, rows, :] = oc.astype(BF16)
+            right[1, side, b, rows, :] = hc.astype(BF16)
             return carry
 
         lax.fori_loop(0, steps, step, 0)
 
-    for b in range(2):
-        m = mask[py * 4 + core * 2 + b].astype(F32)
-        build(
-            lambda rows, b=b: blocks[b, rows, :],
-            lambda rows, b=b: gown[rows, b * BLOCK:(b + 1) * BLOCK],
-            means[py, b, 0:1, :] * m,
-            means[py, b, 1:2, :] * m,
-            m,
-            core * 2 + b,
-        )
-    for copy in pair:
-        copy.wait()
-    for copy in shared:
-        copy.wait()
-    for b in range(2):
-        m = mask[py * 4 + (1 - core) * 2 + b].astype(F32)
-        build(
-            lambda rows, b=b: opar[rows, b * BLOCK:(b + 1) * BLOCK],
-            lambda rows, b=b: gpar[rows, b * BLOCK:(b + 1) * BLOCK],
-            pmeans[b, 0:1, :] * m,
-            pmeans[b, 1:2, :] * m,
-            m,
-            (1 - core) * 2 + b,
-        )
+    def build_own():
+        for b in range(2):
+            m = mask[py * 4 + core * 2 + b].astype(F32)
+            build(
+                lambda rows, b=b: blocks[b, rows, :],
+                lambda rows, b=b: gown[rows, b * BLOCK:(b + 1) * BLOCK],
+                means[py, b, 0:1, :] * m,
+                means[py, b, 1:2, :] * m,
+                m,
+                0,
+                b,
+            )
+
+    def build_partner():
+        for copy in pair:
+            copy.wait()
+        for copy in shared:
+            copy.wait()
+        for b in range(2):
+            m = mask[py * 4 + (1 - core) * 2 + b].astype(F32)
+            build(
+                lambda rows, b=b: opar[rows, b * BLOCK:(b + 1) * BLOCK],
+                lambda rows, b=b: gpar[rows, b * BLOCK:(b + 1) * BLOCK],
+                pmeans[b, 0:1, :] * m,
+                pmeans[b, 1:2, :] * m,
+                m,
+                1,
+                b,
+            )
 
     xs = (px, (wrap4(px + 1) * 4 + pz, pan), (wrap4(px + 3) * 4 + pz, pan))
     zs = (pz, (px * 4 + wrap4(pz + 1), pan), (px * 4 + wrap4(pz + 3), pan))
@@ -178,30 +183,67 @@
             remote(buf.at[1, prv], got.at[5], send.at[5], recv.at[5], down),
         ]
 
-    def ring1_of(r, ch):
-        return ring(part.at[r, ch], ring1.at[r, ch], r1_send.at[r, ch], r1_recv.at[r, ch], (xs, zs)[ch])
-
-    def ring2_of(r, ch):
-        return ring(half.at[r, ch], ring2.at[r, ch], r2_send.at[r, ch], r2_recv.at[r, ch], (zs, xs)[ch])
+    chains = [(ch, side) for side in range(2) for ch in range(2)]
+    arrivals = ((3, 4), (2, 5))
+
+    def ring1_of(r, ch, side):
+        at = (r, ch, side)
+        return ring(part.at[at], ring1.at[at], r1_send.at[at], r1_recv.at[at], (xs, zs)[ch])
+
+    def ring2_of(r, ch, side):
+        at = (r, ch, side)
+        return ring(half.at[at], ring2.at[at], r2_send.at[at], r2_recv.at[at], (zs, xs)[ch])
 
     def ring_start(copies):
         for copy in copies[:4]:
             copy.start()
 
     def ring_mid(copies, buf, got, axis):
-        me = axis[0]
         for b, shift in ((0, 1), (1, 3)):
             copies[b].wait_recv()
-            k = wrap4(me + shift)
+            k = wrap4(axis[0] + shift)
             buf[b, k] = (buf[b, k].astype(F32) + got[b].astype(F32)).astype(BF16)
             copies[4 + b].start()
 
+    def mid1(r, ch, side):
+        at = (r, ch, side)
+        ring_mid(ring1_of(*at), part.at[at], ring1.at[at], (xs, zs)[ch])
+
+    def mid2(r, ch, side):
+        at = (r, ch, side)
+        ring_mid(ring2_of(*at), half.at[at], ring2.at[at], (zs, xs)[ch])
+
+    def reduced(r, ch, side, b, rows):
+        i, j = arrivals[b]
+        own = part[r, ch, side, b, (px, pz)[ch], rows, :].astype(F32)
+        return own + ring1[r, ch, side, i, rows, :].astype(F32) + ring1[r, ch, side, j, rows, :].astype(F32)
+
+    def fin1(r, ch, side):
+        copies = ring1_of(r, ch, side)
+        for b in range(2):
+            for k in arrivals[b]:
+                copies[k].wait_recv()
+            for k in range(4):
+                half[r, ch, side, b, k] = reduced(r, ch, side, b, slice(16 * k, 16 * k + 16)).astype(BF16)
+        ring_start(ring2_of(r, ch, side))
+
+    def fin2(r, ch, side):
+        copies = ring2_of(r, ch, side)
+        for b in range(2):
+            i, j = arrivals[b]
+            copies[i].wait_recv()
+            copies[j].wait_recv()
+            rows = pl.ds(pl.multiple_of((pz, px)[ch] * 16, 16), 16)
+            got = ring2[r, ch, side, i].astype(F32) + ring2[r, ch, side, j].astype(F32)
+            value = (reduced(r, ch, side, b, rows) + got) * scale
+            if side == 0:
+                whole[block_of(r, b), ch] = value
+            else:
+                give[r, b, ch] = value
+
     def source(r, b):
-        second = lax.div(r, 2) * (3 - r)
-        middle = r - second - 3 * lax.div(r, 3)
-        ysrc = wrap4(py + middle * (1 if b else 3) + 2 * lax.div(r, 3))
-        bsel = b + second * (1 - 2 * b)
-        return ysrc, bsel
+        step = ((0, 0), (3, 1), (3, 1), (2, 2))[r][b]
+        return wrap4(py + step), (1 - b if r == 2 else b)
 
     def block_of(r, b):
         ysrc, bsel = source(r, b)
@@ -210,16 +252,13 @@
     def give_copy(r, b):
         return remote(give.at[r, b], whole.at[block_of(r, b)], z_send.at[r, b], z_recv.at[r, b], partner)
 
-    def one_round(r, carry):
-        for t in range(1, ROUNDS):
-
-            @pl.when(r == t)
-            def _():
-                for b in range(2):
-                    gather[2 * (t - 1) + b].wait_recv()
-                    if t == 1:
-                        gather[4 + b].start()
-
+    def gathered(r):
+        for b in range(2):
+            gather[2 * (r - 1) + b].wait_recv()
+            if r == 1:
+                gather[4 + b].start()
+
+    def load_left(r):
         for b in range(2):
             ysrc, bsel = source(r, b)
             m = mask[ysrc * 4 + core * 2 + bsel].astype(F32)
@@ -233,59 +272,59 @@
 
             lax.fori_loop(0, steps, turn, 0)
 
-        for ch in range(2):
-            for tile in range(4):
-                product = jnp.dot(left_t[...], right[ch, tile], preferred_element_type=F32)
-                h, off = tile // 2, (tile % 2) * BLOCK
-                part[r, ch, :, :, h, :, off:off + BLOCK] = product.astype(BF16).reshape(2, 4, 64, BLOCK)
-            ring_start(ring1_of(r, ch))
-
-        for ch in range(2):
-            ring_mid(ring1_of(r, ch), part.at[r, ch], ring1.at[r, ch], (xs, zs)[ch])
-        for ch in range(2):
-            copies = ring1_of(r, ch)
-            me = (px, pz)[ch]
-            for b, (i, j) in enumerate(((3, 4), (2, 5))):
-                copies[i].wait_recv()
-                copies[j].wait_recv()
-                for k in range(4):
-                    rows = slice(16 * k, 16 * k + 16)
-                    value = (
-                        part[r, ch, b, me, :, rows, :].astype(F32)
-                        + ring1[r, ch, i, :, rows, :].astype(F32)
-                        + ring1[r, ch, j, :, rows, :].astype(F32)
-                    )
-                    half[r, ch, b, k] = value.astype(BF16)
-            ring_start(ring2_of(r, ch))
-        for ch in range(2):
-            ring_mid(ring2_of(r, ch), half.at[r, ch], ring2.at[r, ch], (zs, xs)[ch])
-        for b, (i, j) in enumerate(((3, 4), (2, 5))):
-            for ch in range(2):
-                copies = ring2_of(r, ch)
-                me = (pz, px)[ch]
-                copies[i].wait_recv()
-                copies[j].wait_recv()
-
-                def value(h):
-                    return (
-                        half[r, ch, b, me, h].astype(F32)
-                        + ring2[r, ch, i, h].astype(F32)
-                        + ring2[r, ch, j, h].astype(F32)
-                    ) * scale
-
-                whole[block_of(r, b), ch] = value(core)
-                give[r, b, ch] = value(1 - core)
+    def multiply(r, ch, side):
+        for b in range(2):
+            product = jnp.dot(left_t[...], right[ch, side, b], preferred_element_type=F32)
+            part[r, ch, side, :, :, :, b * BLOCK:(b + 1) * BLOCK] = product.astype(BF16).reshape(2, 4, 64, BLOCK)
+        ring_start(ring1_of(r, ch, side))
+
+    def finish(r):
+        for ch, side in chains:
+            fin2(r, ch, side)
+        for b in range(2):
             give_copy(r, b).start()
-        return carry
-
-    lax.fori_loop(0, ROUNDS, one_round, 0)
-
-    def give_wait(r, carry):
+
+    build_own()
+    load_left(0)
+    multiply(0, 0, 0)
+    multiply(0, 1, 0)
+    build_partner()
+    multiply(0, 0, 1)
+    multiply(0, 1, 1)
+    for r in range(1, ROUNDS):
+        if r > 1:
+            for ch, side in chains:
+                mid1(r - 1, ch, side)
+            for ch, side in chains:
+                fin1(r - 1, ch, side)
+        gathered(r)
+        load_left(r)
+        multiply(r, 0, 0)
+        if r == 1:
+            for ch, side in chains:
+                mid1(r - 1, ch, side)
+        else:
+            for ch, side in chains:
+                mid2(r - 1, ch, side)
+        multiply(r, 1, 0)
+        if r == 1:
+            for ch, side in chains:
+                fin1(r - 1, ch, side)
+        multiply(r, 0, 1)
+        if r == 1:
+            for ch, side in chains:
+                mid2(r - 1, ch, side)
+        multiply(r, 1, 1)
+        finish(r - 1)
+    last = ROUNDS - 1
+    for step in (mid1, fin1, mid2):
+        for ch, side in chains:
+            step(last, ch, side)
+    finish(last)
+
+    for r in range(ROUNDS):
         for b in range(2):
             give_copy(r, b).wait()
-        return carry
-
-    lax.fori_loop(0, ROUNDS, give_wait, 0)
 
     row_c = pl.multiple_of(px * 64 + pz * 16, 16)
     row_h = pl.multiple_of(pz * 64 + px * 16, 16)
@@ -294,7 +333,7 @@
         return [
             remote(
                 staged.at[r, ch],
-                (out_c, out_h)[ch].at[pl.ds((row_c, row_h)[ch], 16), :],
+                out.at[ch, pl.ds((row_c, row_h)[ch], 16), :],
                 f_send.at[d, ch],
                 f_recv.at[d, ch],
                 (r, pan),
@@ -304,7 +343,7 @@
 
     def place_start(d, carry):
         r = lax.rem(walk + d, 16)
-        staged[r] = whole[owner[r]]
+        staged[r] = whole[owner[r]].astype(BF16)
         for copy in place(r, d):
             copy.start()
         return carry
@@ -315,10 +354,10 @@
         return carry
 
     lax.fori_loop(1, 16, place_start, 0)
-    staged[walk] = whole[owner[walk]]
+    staged[walk] = whole[owner[walk]].astype(BF16)
     mine = [
         pltpu.make_async_copy(
-            staged.at[walk, ch], (out_c, out_h)[ch].at[pl.ds((row_c, row_h)[ch], 16), :], local_sem.at[ch]
+            staged.at[walk, ch], out.at[ch, pl.ds((row_c, row_h)[ch], 16), :], local_sem.at[ch]
         )
         for ch in range(2)
     ]
@@ -328,8 +367,8 @@
         copy.wait_send()
 
     def sends(r, carry):
-        for ch in range(2):
-            for copy in ring1_of(r, ch) + ring2_of(r, ch):
+        for ch, side in chains:
+            for copy in ring1_of(r, ch, side) + ring2_of(r, ch, side):
                 copy.wait_send()
         return carry
 
@@ -344,38 +383,38 @@
     anywhere = pl.BlockSpec(memory_space=pl.ANY)
     scalars = pl.BlockSpec(memory_space=pltpu.SMEM)
     dma = pltpu.SemaphoreType.DMA
-    out = jax.ShapeDtypeStruct((BLOCK, width), F32)
-    return pl.pallas_call(
+    both = pl.pallas_call(
         kernel,
-        out_shape=(out, out),
+        out_shape=jax.ShapeDtypeStruct((2, BLOCK, width), BF16),
         in_specs=[scalars, scalars, anywhere, anywhere, pl.BlockSpec(memory_space=pltpu.VMEM)],
-        out_specs=(anywhere, anywhere),
+        out_specs=anywhere,
         scratch_shapes=[
             pltpu.VMEM((8, walkers, BLOCK), BF16),
             pltpu.VMEM((walkers, width), BF16),
             pltpu.VMEM((walkers, width), BF16),
             pltpu.VMEM((walkers, width), BF16),
-            pltpu.VMEM((2, 4, walkers, BLOCK), BF16),
+            pltpu.VMEM((2, 2, 2, walkers, BLOCK), BF16),
             pltpu.VMEM((2 * BLOCK, walkers), BF16),
             pltpu.VMEM((walkers, 128), F32),
-            pltpu.VMEM((ROUNDS, 2, 2, 4, 2, 64, width), BF16),
-            pltpu.VMEM((ROUNDS, 2, 6, 2, 64, width), BF16),
-            pltpu.VMEM((ROUNDS, 2, 2, 4, 2, 16, width), BF16),
-            pltpu.VMEM((ROUNDS, 2, 6, 2, 16, width), BF16),
+            pltpu.VMEM((ROUNDS, 2, 2, 2, 4, 64, width), BF16),
+            pltpu.VMEM((ROUNDS, 2, 2, 6, 64, width), BF16),
+            pltpu.VMEM((ROUNDS, 2, 2, 2, 4, 16, width), BF16),
+            pltpu.VMEM((ROUNDS, 2, 2, 6, 16, width), BF16),
             pltpu.VMEM((16, 2, 16, width), F32),
             pltpu.VMEM((ROUNDS, 2, 2, 16, width), F32),
-            pltpu.VMEM((16, 2, 16, width), F32),
+            pltpu.VMEM((16, 2, 16, width), BF16),
             pltpu.VMEM((16, 2, 8, BLOCK), F32),
             pltpu.VMEM((4, 2, 8, BLOCK), F32),
             pltpu.VMEM((2, 8, BLOCK), F32),
             dma((3,)), dma((6,)), dma((6,)), dma((2,)), dma((2,)), dma((16,)), dma((16,)), dma((4,)), dma((4,)),
-            dma((ROUNDS, 2, 6)), dma((ROUNDS, 2, 6)), dma((ROUNDS, 2, 6)), dma((ROUNDS, 2, 6)),
+            dma((ROUNDS, 2, 2, 6)), dma((ROUNDS, 2, 2, 6)), dma((ROUNDS, 2, 2, 6)), dma((ROUNDS, 2, 2, 6)),
             dma((ROUNDS, 2)), dma((ROUNDS, 2)), dma((16, 2)), dma((16, 2)),
         ],
         compiler_params=pltpu.CompilerParams(
             collective_id=0, has_side_effects=True, vmem_limit_bytes=64 * 1000 * 1000
         ),
     )(mask, owner, dlog, dener, energy.reshape(walkers // 128, 128))
+    return both[0].astype(F32), both[1].astype(F32)
 
 
 def solution(mesh):

time: 176 us -> 138 us (0.78); the launches traced: 173 us -> 138 us
  Pallas kernels: 168 us -> 135 us
  local copies, waits for them, and re-layouts: 3.74 us -> 0 us
  other arithmetic: 0 us -> 2.13 us
    pallas_call x1, Pallas kernels: 168 us -> 135 us  [per_device(): pl.pallas_call(kernel, out_shape=jax.ShapeDtypeStruct((2, BLOCK, width),...]
    unnamed x2 -> x0, local copies, waits for them, and re-layouts: 3.74 us -> none
    convert_element_type x0 -> x1, other arithmetic: none -> 2.13 us  [per_device(): return (both[0].astype(F32), both[1].astype(F32))]
where the time goes in v2:
time: 138 us
  Pallas kernels  135 us (98%)
  other arithmetic  2.13 us (2%)
    pallas_call x1, Pallas kernels, per_device(): pl.pallas_call(kernel, out_shape=jax.ShapeDtypeStruct((2, BLOCK, width),...  135 us

profile of v2, /device:TPU:1, one launch (start us, length us, event | category | flops | bytes accessed | tf_op | source)
XLA Modules:
  0.0 137.7 jit_solution(800667390173051565)
XLA Ops:
  0.6 134.9 %shard_map.68 = bf16[2,256,512]{2,1,0:T(8,128)(2,1)} custom-call(s32[16]{0:T(128)} %mask.1, s32[16]{0:T(128)} %owner.1, bf16[2048,512]{1,0:T(8,128)(2,1)} %dlog.1, bf16[2048,512]{1,0:T(8,128)(2,1)} %dener.1, f32[16,128]{1,0:T(8,128)} %bitcast.7), custom_call_target="tpu_custom_call" | custom-call | tf_op jit(solution)/shard_map/pallas_call | solution.py:386
  135.5 2.1 %bitcast_convert_fusion = (f32[256,512]{1,0:T(8,128)}, f32[256,512]{1,0:T(8,128)}) fusion(bf16[2,256,512]{2,1,0:T(8,128)(2,1)} %shard_map.68), kind=kLoop, calls=%fused_computation | loop fusion | flops 262144 | bytes 1572864 | tf_op jit(solution)/shard_map/convert_element_type | solution.py:417

commit v3 on v2

--- a/solution.py
+++ b/solution.py
@@ -51,15 +51,18 @@
 
     barrier = pltpu.get_barrier_semaphore()
 
-    def greet(d, carry):
-        pl.semaphore_signal(barrier, inc=1, device_id=(lax.rem(walk + d, 16), pan), device_id_type=MESH)
-        return carry
-
-    lax.fori_loop(1, 16, greet, 0)
-    for d in range(1, 4):
-        pl.semaphore_signal(barrier, inc=1, device_id=at_y(d), device_id_type=MESH)
-    pl.semaphore_signal(barrier, inc=1, device_id=partner, device_id_type=MESH)
-    pl.semaphore_wait(barrier, 19)
+    near = [
+        (wrap4(px + 1) * 4 + pz, pan),
+        (wrap4(px + 3) * 4 + pz, pan),
+        (px * 4 + wrap4(pz + 1), pan),
+        (px * 4 + wrap4(pz + 3), pan),
+        at_y(1),
+        at_y(3),
+        partner,
+    ]
+    for device in near:
+        pl.semaphore_signal(barrier, inc=1, device_id=device, device_id_type=MESH)
+    pl.semaphore_wait(barrier, len(near))
 
     def column(b):
         return dlog.at[:, pl.ds(b * BLOCK, BLOCK)]
@@ -72,7 +75,7 @@
         remote(blocks.at[2], blocks.at[6], ag_send.at[4], ag_recv.at[4], at_y(1)),
         remote(blocks.at[3], blocks.at[7], ag_send.at[5], ag_recv.at[5], at_y(3)),
     ]
-    for copy in gather[:4]:
+    for copy in gather[:2]:
         copy.start()
     pair = [
         remote(dlog, opar, pt_send.at[0], pt_recv.at[0], partner),
@@ -94,31 +97,28 @@
 
         zero = jnp.zeros((1, BLOCK), F32)
         o, g = lax.fori_loop(0, steps, add, (zero, zero))
-        stats[walk, b] = jnp.concatenate([o, g, jnp.full((1, BLOCK), esum, F32), jnp.zeros((5, BLOCK), F32)], axis=0)
-
-    def stat_copy(d):
-        return remote(
-            stats.at[walk], stats.at[walk], st_send.at[d], st_recv.at[d], (lax.rem(walk + d, 16), pan)
-        )
-
-    def stat_start(d, carry):
-        stat_copy(d).start()
-        return carry
-
-    def stat_wait(d, carry):
-        stat_copy(d).wait()
-        return carry
-
-    lax.fori_loop(1, 16, stat_start, 0)
-    lax.fori_loop(1, 16, stat_wait, 0)
-    sums = stats[0]
-    for i in range(1, 16):
-        sums = sums + stats[i]
-    means[py] = sums * scale
-    shared = [remote(means.at[py], means.at[py], mm_send.at[d], mm_recv.at[d], at_y(d)) for d in range(1, 4)] + [
-        remote(means.at[py], pmeans, mm_send.at[0], mm_recv.at[0], partner)
-    ]
-    for copy in shared:
+        stats[0, 0, b] = jnp.concatenate([o, g, jnp.full((1, BLOCK), esum, F32), jnp.zeros((5, BLOCK), F32)], axis=0)
+
+    swaps = [
+        ((px + 1 - 2 * lax.rem(px, 2)) * 4 + pz, pan),
+        ((3 - px) * 4 + pz, pan),
+        (px * 4 + pz + 1 - 2 * lax.rem(pz, 2), pan),
+        (px * 4 + 3 - pz, pan),
+    ]
+    for n, device in enumerate(swaps):
+        swap = remote(stats.at[0, n], stats.at[1, n], st_send.at[n], st_recv.at[n], device)
+        swap.start()
+        swap.wait()
+        stats[0, n + 1] = stats[0, n] + stats[1, n]
+    means[py] = stats[0, 4] * scale
+    below = wrap4(py + 3)
+    shared = [
+        remote(means.at[py], means.at[py], mm_send.at[0], mm_recv.at[0], at_y(1)),
+        remote(means.at[py], means.at[py], mm_send.at[1], mm_recv.at[1], at_y(3)),
+        remote(means.at[below], means.at[below], mm_send.at[2], mm_recv.at[2], at_y(1)),
+        remote(means.at[py], pmeans, mm_send.at[3], mm_recv.at[3], partner),
+    ]
+    for copy in [shared[0], shared[1], shared[3]] + gather[2:4]:
         copy.start()
 
     ebar = means[py, 0, 2:3, 0:128]
@@ -154,8 +154,7 @@
     def build_partner():
         for copy in pair:
             copy.wait()
-        for copy in shared:
-            copy.wait()
+        shared[3].wait()
         for b in range(2):
             m = mask[py * 4 + (1 - core) * 2 + b].astype(F32)
             build(
@@ -253,6 +252,10 @@
         return remote(give.at[r, b], whole.at[block_of(r, b)], z_send.at[r, b], z_recv.at[r, b], partner)
 
     def gathered(r):
+        for k in ((0, 1), (), (2,))[r - 1]:
+            shared[k].wait_recv()
+        if r == 1:
+            shared[2].start()
         for b in range(2):
             gather[2 * (r - 1) + b].wait_recv()
             if r == 1:
@@ -363,7 +366,7 @@
     ]
     for copy in mine:
         copy.start()
-    for copy in gather:
+    for copy in gather + shared[:3]:
         copy.wait_send()
 
     def sends(r, carry):
@@ -403,10 +406,10 @@
             pltpu.VMEM((16, 2, 16, width), F32),
             pltpu.VMEM((ROUNDS, 2, 2, 16, width), F32),
             pltpu.VMEM((16, 2, 16, width), BF16),
-            pltpu.VMEM((16, 2, 8, BLOCK), F32),
+            pltpu.VMEM((2, 5, 2, 8, BLOCK), F32),
             pltpu.VMEM((4, 2, 8, BLOCK), F32),
             pltpu.VMEM((2, 8, BLOCK), F32),
-            dma((3,)), dma((6,)), dma((6,)), dma((2,)), dma((2,)), dma((16,)), dma((16,)), dma((4,)), dma((4,)),
+            dma((3,)), dma((6,)), dma((6,)), dma((2,)), dma((2,)), dma((4,)), dma((4,)), dma((4,)), dma((4,)),
             dma((ROUNDS, 2, 2, 6)), dma((ROUNDS, 2, 2, 6)), dma((ROUNDS, 2, 2, 6)), dma((ROUNDS, 2, 2, 6)),
             dma((ROUNDS, 2)), dma((ROUNDS, 2)), dma((16, 2)), dma((16, 2)),
         ],

time: 138 us -> 117 us (0.85)
  Pallas kernels: 135 us -> 114 us
    pallas_call x1, Pallas kernels: 135 us -> 114 us  [per_device(): pl.pallas_call(kernel, out_shape=jax.ShapeDtypeStruct((2, BLOCK, width),...]
where the time goes in v3:
time: 117 us; the launch traced here: 116 us
  Pallas kernels  114 us (97%)
  other arithmetic  2.13 us (2%)
    pallas_call x1, Pallas kernels, per_device(): pl.pallas_call(kernel, out_shape=jax.ShapeDtypeStruct((2, BLOCK, width),...  114 us

profile of v3, /device:TPU:1, one launch (start us, length us, event | category | flops | bytes accessed | tf_op | source)
XLA Modules:
  0.0 116.4 jit_solution(1606458899618822781)
XLA Ops:
  0.6 113.6 %shard_map.68 = bf16[2,256,512]{2,1,0:T(8,128)(2,1)} custom-call(s32[16]{0:T(128)} %mask.1, s32[16]{0:T(128)} %owner.1, bf16[2048,512]{1,0:T(8,128)(2,1)} %dlog.1, bf16[2048,512]{1,0:T(8,128)(2,1)} %dener.1, f32[16,128]{1,0:T(8,128)} %bitcast.7), custom_call_target="tpu_custom_call" | custom-call | tf_op jit(solution)/shard_map/pallas_call | solution.py:389
  114.2 2.1 %bitcast_convert_fusion = (f32[256,512]{1,0:T(8,128)}, f32[256,512]{1,0:T(8,128)}) fusion(bf16[2,256,512]{2,1,0:T(8,128)(2,1)} %shard_map.68), kind=kLoop, calls=%fused_computation | loop fusion | flops 262144 | bytes 1572864 | tf_op jit(solution)/shard_map/convert_element_type | solution.py:420

commit v4 on v3

v4 whole, which is shorter than its diff:
```python
import jax
import jax.numpy as jnp
from jax import lax
from jax.experimental import pallas as pl
from jax.experimental.pallas import tpu as pltpu
from jax.sharding import PartitionSpec as P

BLOCK = 256
ROUNDS = 5
PAIRS = 3
MESH = pl.DeviceIdType.MESH
F32 = jnp.float32
BF16 = jnp.bfloat16


def wrap4(v):
    return lax.rem(v, 4)


def kernel(
    mask_in, owner_in, dlog, dener, energy_in, out,
    mask, owner, energy,
    blocks, gown, opar, gpar, right, left_t, spread,
    part, ring1, half, ring2, part_s, ring1_s, half_s, ring2_s,
    near2, cross2, whole_c, whole_h, give, staged, stats, means, pmeans,
    local_sem, ag_send, ag_recv, pt_send, pt_recv, st_send, st_recv, mm_send, mm_recv,
    r1_send, r1_recv, r2_send, r2_recv, z_send, z_recv, f_send, f_recv,
    n2_send, n2_recv, c2_send, c2_recv,
):
    walkers = dlog.shape[0]
    total = walkers * 16
    scale = 1.0 / total
    chunk = 256
    steps = walkers // chunk

    walk = lax.axis_index("walk")
    pan = lax.axis_index("pan")
    px, pz = lax.div(walk, 4), lax.rem(walk, 4)
    py, core = lax.div(pan, 2), lax.rem(pan, 2)
    partner = (walk, py * 2 + (1 - core))

    def at_y(shift):
        return (walk, wrap4(py + shift) * 2 + core)

    def remote(src, dst, send, recv, device):
        return pltpu.make_async_remote_copy(
            src_ref=src, dst_ref=dst, send_sem=send, recv_sem=recv, device_id=device, device_id_type=MESH
        )

    barrier = pltpu.get_barrier_semaphore()

    near = [
        (wrap4(px + 1) * 4 + pz, pan),
        (wrap4(px + 3) * 4 + pz, pan),
        (px * 4 + wrap4(pz + 1), pan),
        (px * 4 + wrap4(pz + 3), pan),
        at_y(1),
        at_y(3),
        partner,
    ]
    for device in near:
        pl.semaphore_signal(barrier, inc=1, device_id=device, device_id_type=MESH)
    small = [
        pltpu.make_async_copy(source, target, local_sem.at[3 + n])
        for n, (source, target) in enumerate(((mask_in, mask), (owner_in, owner), (energy_in, energy)))
    ]
    own = [
        pltpu.make_async_copy(dlog.at[:, pl.ds(b * BLOCK, BLOCK)], blocks.at[b], local_sem.at[b]) for b in range(2)
    ] + [pltpu.make_async_copy(dener, gown, local_sem.at[2])]
    pl.semaphore_wait(barrier, len(near))

    def column(b):
        return dlog.at[:, pl.ds(b * BLOCK, BLOCK)]

    def onward(n, slot, to):
        rows = pl.ds((slot % 2) * (walkers // 2), walkers // 2)
        return remote(
            blocks.at[slot, rows, :], blocks.at[to, rows, :], ag_send.at[n], ag_recv.at[n], at_y(3 if slot % 2 else 1)
        )

    gather = [
        remote(column(0), blocks.at[2], ag_send.at[0], ag_recv.at[0], at_y(1)),
        remote(column(0), blocks.at[3], ag_send.at[1], ag_recv.at[1], at_y(3)),
        remote(column(1), blocks.at[4], ag_send.at[2], ag_recv.at[2], at_y(1)),
        remote(column(1), blocks.at[5], ag_send.at[3], ag_recv.at[3], at_y(3)),
        onward(4, 2, 6),
        onward(5, 3, 6),
        onward(6, 4, 7),
        onward(7, 5, 7),
    ]
    for copy in gather[:2] + own + small:
        copy.start()
    pair = [
        remote(dlog, opar, pt_send.at[0], pt_recv.at[0], partner),
        remote(dener, gpar, pt_send.at[1], pt_recv.at[1], partner),
    ]
    for copy in pair:
        copy.start()

    for copy in own + small:
        copy.wait()
    esum = jnp.sum(energy[...])
    for b in range(2):

        def add(i, carry):
            rows = pl.ds(pl.multiple_of(i * chunk, chunk), chunk)
            o = jnp.sum(blocks[b, rows, :].astype(F32), axis=0, keepdims=True)
            g = jnp.sum(gown[rows, b * BLOCK:(b + 1) * BLOCK].astype(F32), axis=0, keepdims=True)
            return carry[0] + o, carry[1] + g

        zero = jnp.zeros((1, BLOCK), F32)
        o, g = lax.fori_loop(0, steps, add, (zero, zero))
        stats[0, 0, b] = jnp.concatenate([o, g, jnp.full((1, BLOCK), esum, F32), jnp.zeros((5, BLOCK), F32)], axis=0)

    swaps = [
        ((px + 1 - 2 * lax.rem(px, 2)) * 4 + pz, pan),
        ((3 - px) * 4 + pz, pan),
        (px * 4 + pz + 1 - 2 * lax.rem(pz, 2), pan),
        (px * 4 + 3 - pz, pan),
    ]
    for n, device in enumerate(swaps):
        swap = remote(stats.at[0, n], stats.at[1, n], st_send.at[n], st_recv.at[n], device)
        swap.start()
        swap.wait()
        stats[0, n + 1] = stats[0, n] + stats[1, n]
    means[py] = stats[0, 4] * scale
    below = wrap4(py + 3)
    shared = [
        remote(means.at[py], means.at[py], mm_send.at[0], mm_recv.at[0], at_y(1)),
        remote(means.at[py], means.at[py], mm_send.at[1], mm_recv.at[1], at_y(3)),
        remote(means.at[below], means.at[below], mm_send.at[2], mm_recv.at[2], at_y(1)),
        remote(means.at[py], pmeans, mm_send.at[3], mm_recv.at[3], partner),
    ]
    for copy in [shared[0], shared[1], shared[3]] + gather[2:4]:
        copy.start()

    ebar = means[py, 0, 2:3, 0:128]
    for i in range(walkers // 128):
        row = energy[i:i + 1, :] - ebar
        spread[i * 128:(i + 1) * 128, :] = jnp.broadcast_to(row, (128, 128)).T

    def build(o_of, g_of, obar, gbar, m, side, b):
        def step(i, carry):
            rows = pl.ds(pl.multiple_of(i * chunk, chunk), chunk)
            oc = o_of(rows).astype(F32) * m - obar
            e = spread[rows, :]
            hc = jnp.concatenate([e, e], axis=1) * oc + g_of(rows).astype(F32) * m - gbar
            right[0, side, b, rows, :] = oc.astype(BF16)
            right[1, side, b, rows, :] = hc.astype(BF16)
            return carry

        lax.fori_loop(0, steps, step, 0)

    def build_own():
        for b in range(2):
            m = mask[py * 4 + core * 2 + b].astype(F32)
            build(
                lambda rows, b=b: blocks[b, rows, :],
                lambda rows, b=b: gown[rows, b * BLOCK:(b + 1) * BLOCK],
                means[py, b, 0:1, :] * m,
                means[py, b, 1:2, :] * m,
                m,
                0,
                b,
            )

    def build_partner():
        for copy in pair:
            copy.wait()
        shared[3].wait()
        for b in range(2):
            m = mask[py * 4 + (1 - core) * 2 + b].astype(F32)
            build(
                lambda rows, b=b: opar[rows, b * BLOCK:(b + 1) * BLOCK],
                lambda rows, b=b: gpar[rows, b * BLOCK:(b + 1) * BLOCK],
                pmeans[b, 0:1, :] * m,
                pmeans[b, 1:2, :] * m,
                m,
                1,
                b,
            )

    xs = (px, (wrap4(px + 1) * 4 + pz, pan), (wrap4(px + 3) * 4 + pz, pan))
    zs = (pz, (px * 4 + wrap4(pz + 1), pan), (px * 4 + wrap4(pz + 3), pan))

    def ring(buf, got, send, recv, axis):
        me, up, down = axis
        far, nxt, prv = wrap4(me + 2), wrap4(me + 1), wrap4(me + 3)
        return [
            remote(buf.at[0, far], got.at[0], send.at[0], recv.at[0], up),
            remote(buf.at[1, far], got.at[1], send.at[1], recv.at[1], down),
            remote(buf.at[1, nxt], got.at[2], send.at[2], recv.at[2], up),
            remote(buf.at[0, prv], got.at[3], send.at[3], recv.at[3], down),
            remote(buf.at[0, nxt], got.at[4], send.at[4], recv.at[4], up),
            remote(buf.at[1, prv], got.at[5], send.at[5], recv.at[5], down),
        ]

    last = ROUNDS - 1
    chains = [(ch, side) for side in range(2) for ch in range(2)]
    arrivals = ((3, 4), (2, 5))

    def buffers(r):
        return (part, ring1, half, ring2, r) if r < PAIRS else (part_s, ring1_s, half_s, ring2_s, r - PAIRS)

    def ring1_of(r, ch, side):
        buf, got, _, _, n = buffers(r)
        sems = (r, ch, side)
        return ring(buf.at[n, ch, side], got.at[n, ch, side], r1_send.at[sems], r1_recv.at[sems], (xs, zs)[ch])

    def ring2_of(r, ch, side):
        _, _, buf, got, n = buffers(r)
        sems = (r, ch, side)
        return ring(buf.at[n, ch, side], got.at[n, ch, side], r2_send.at[sems], r2_recv.at[sems], (zs, xs)[ch])

    def ring_start(copies):
        for copy in copies[:4]:
            copy.start()

    def ring_mid(copies, buf, got, axis):
        for b, shift in ((0, 1), (1, 3)):
            copies[b].wait_recv()
            k = wrap4(axis[0] + shift)
            buf[b, k] = (buf[b, k].astype(F32) + got[b].astype(F32)).astype(BF16)
            copies[4 + b].start()

    def mid1(r, ch, side):
        buf, got, _, _, n = buffers(r)
        ring_mid(ring1_of(r, ch, side), buf.at[n, ch, side], got.at[n, ch, side], (xs, zs)[ch])

    def mid2(r, ch, side):
        _, _, buf, got, n = buffers(r)
        ring_mid(ring2_of(r, ch, side), buf.at[n, ch, side], got.at[n, ch, side], (zs, xs)[ch])

    def reduced(r, ch, side, b, rows):
        buf, got, _, _, n = buffers(r)
        i, j = arrivals[b]
        own = buf[n, ch, side, b, (px, pz)[ch], rows, :].astype(F32)
        return own + got[n, ch, side, i, rows, :].astype(F32) + got[n, ch, side, j, rows, :].astype(F32)

    def fin1(r, ch, side):
        copies = ring1_of(r, ch, side)
        _, _, buf, _, n = buffers(r)
        for b in range(2):
            for k in arrivals[b]:
                copies[k].wait_recv()
            for k in range(4):
                buf[n, ch, side, b, k] = reduced(r, ch, side, b, slice(16 * k, 16 * k + 16)).astype(BF16)
        if r < last:
            ring_start(ring2_of(r, ch, side))
        else:
            for copy in direct2(ch, side):
                copy.start()

    def direct2(ch, side):
        me = (pz, px)[ch]
        copies = []
        for d in range(1 - side, 4):
            k = wrap4(me + d)
            device = ((px * 4 + k, k * 4 + pz)[ch], py * 2 + (1 - core if side else core))
            copies.append(
                remote(
                    half_s.at[last - PAIRS, ch, side, :, k],
                    (near2, cross2)[side].at[ch, d],
                    (n2_send, c2_send)[side].at[ch, d],
                    (n2_recv, c2_recv)[side].at[ch, d],
                    device,
                )
            )
        return copies

    def fin2_last(ch):
        order = last + PAIRS
        ysrc, bsel = source(order)
        rows = pl.ds(pl.multiple_of((pz, px)[ch] * 16, 16), 16)
        for side in range(2):
            for copy in direct2(ch, side):
                copy.wait_recv()
            for b in range(2):
                value = near2[ch, 1, b].astype(F32) if side == 0 else cross2[ch, 1, b].astype(F32)
                for d in (2, 3):
                    value = value + (near2, cross2)[side][ch, d, b].astype(F32)
                value = value + (reduced(last, ch, 0, b, rows) if side == 0 else cross2[ch, 0, b].astype(F32))
                block = ysrc * 4 + (1 - core if side else core) * 2 + bsel
                whole[ch][block, :, b * BLOCK:(b + 1) * BLOCK] = value * scale

    def fin2(r, ch, side):
        copies = ring2_of(r, ch, side)
        _, _, _, ring, n = buffers(r)
        for b in range(2):
            i, j = arrivals[b]
            copies[i].wait_recv()
            copies[j].wait_recv()
            rows = pl.ds(pl.multiple_of((pz, px)[ch] * 16, 16), 16)
            got = ring[n, ch, side, i].astype(F32) + ring[n, ch, side, j].astype(F32)
            value = (reduced(r, ch, side, b, rows) + got) * scale
            order = 2 * r + b if r < PAIRS else r + PAIRS
            lanes = slice(0, 2 * BLOCK) if r < PAIRS else slice(b * BLOCK, (b + 1) * BLOCK)
            if side == 0:
                whole[ch][block_of(order), :, lanes] = value
            else:
                give[order, ch, :, lanes] = value

    whole = (whole_c, whole_h)
    meets = ((0, 0), (0, 1), (3, 0), (1, 0), (3, 1), (1, 1), (2, 0), (2, 1))

    def source(order):
        return wrap4(py + meets[order][0]), meets[order][1]

    def block_of(order):
        ysrc, bsel = source(order)
        return ysrc * 4 + core * 2 + bsel

    def orders(r):
        return (2 * r, 2 * r + 1) if r < PAIRS else (r + PAIRS,)

    def give_copy(order, ch):
        return remote(
            give.at[order, ch], whole[ch].at[block_of(order)], z_send.at[order, ch], z_recv.at[order, ch], partner
        )

    def gathered(r):
        for k in ((0, 1), (), (2,), ())[r - 1]:
            shared[k].wait_recv()
        if r == 1:
            shared[2].start()
        for b in range(2):
            gather[2 * (r - 1) + b].wait_recv()
            if r <= 2:
                gather[2 * (r + 1) + b].start()

    def load_left(r):
        for b, order in enumerate(orders(r)):
            ysrc, bsel = source(order)
            m = mask[ysrc * 4 + core * 2 + bsel].astype(F32)
            obar = means[ysrc, bsel, 0:1, :] * m

            def turn(i, c):
                rows = pl.ds(pl.multiple_of(i * chunk, chunk), chunk)
                oc = blocks[order, rows, :].astype(F32) * m - obar
                left_t[b * BLOCK:(b + 1) * BLOCK, rows] = oc.T.astype(BF16)
                return c

            lax.fori_loop(0, steps, turn, 0)

    def multiply(r, ch, side):
        for b in range(2):
            if r < PAIRS:
                product = jnp.dot(left_t[...], right[ch, side, b], preferred_element_type=F32).astype(BF16)
                part[r, ch, side, :, :, :, b * BLOCK:(b + 1) * BLOCK] = product.reshape(2, 4, 64, BLOCK)
            else:
                product = jnp.dot(left_t[:BLOCK, :], right[ch, side, b], preferred_element_type=F32).astype(BF16)
                part_s[r - PAIRS, ch, side, b] = product.reshape(4, 64, BLOCK)
        ring_start(ring1_of(r, ch, side))

    def finish(r, ch):
        for side in range(2):
            fin2(r, ch, side)
        for order in orders(r):
            give_copy(order, ch).start()

    build_own()
    load_left(0)
    multiply(0, 0, 0)
    multiply(0, 1, 0)
    build_partner()
    multiply(0, 0, 1)
    multiply(0, 1, 1)
    def every(step, r):
        for ch, side in chains:
            step(r, ch, side)

    def finish_both(r):
        finish(r, 0)
        finish(r, 1)

    between = {
        1: (lambda: every(mid1, 0), None, lambda: every(fin1, 0), None),
        2: (lambda: every(mid2, 1), None, lambda: finish_both(1), None),
        3: (None, None, None, None),
        4: (lambda: every(mid2, 2), lambda: every(fin1, 3), lambda: finish_both(2), None),
    }
    after = {
        1: ((every, mid2, 0), (finish_both, 0), (every, mid1, 1), (every, fin1, 1)),
        2: (),
        3: ((every, mid1, 2), (every, fin1, 2), (every, mid1, 3)),
        4: ((every, mid1, 4), (every, mid2, 3)),
    }
    for r in range(1, ROUNDS):
        gathered(r)
        load_left(r)
        for (ch, side), also in zip(((0, 0), (0, 1), (1, 0), (1, 1)), between[r]):
            multiply(r, ch, side)
            if also is not None:
                also()
        for call, *arguments in after[r]:
            call(*arguments)

    row_c = pl.multiple_of(px * 64 + pz * 16, 16)
    row_h = pl.multiple_of(pz * 64 + px * 16, 16)

    def place(r, d, ch):
        return remote(
            staged.at[ch, r],
            out.at[ch, pl.ds((row_c, row_h)[ch], 16), :],
            f_send.at[d, ch],
            f_recv.at[d, ch],
            (r, pan),
        )

    mine = [
        pltpu.make_async_copy(
            staged.at[ch, walk], out.at[ch, pl.ds((row_c, row_h)[ch], 16), :], local_sem.at[ch]
        )
        for ch in range(2)
    ]

    def place_start(ch):
        for order in range(last + PAIRS):
            give_copy(order, ch).wait()

        def step(d, carry):
            r = lax.rem(walk + d, 16)
            staged[ch, r] = whole[ch][owner[r]].astype(BF16)
            place(r, d, ch).start()
            return carry

        lax.fori_loop(1, 16, step, 0)
        staged[ch, walk] = whole[ch][owner[walk]].astype(BF16)
        mine[ch].start()

    def place_wait(ch):
        def step(d, carry):
            place(lax.rem(walk + d, 16), d, ch).wait()
            return carry

        lax.fori_loop(1, 16, step, 0)

    by_output = [(0, 0), (0, 1), (1, 0), (1, 1)]
    for ch, side in by_output:
        fin1(last, ch, side)
    finish_both(last - 1)
    for ch in range(2):
        fin2_last(ch)
        place_start(ch)
    for copy in gather + shared[:3]:
        copy.wait_send()

    for r in range(ROUNDS):
        for ch, side in chains:
            for copy in ring1_of(r, ch, side) + (ring2_of(r, ch, side) if r < last else direct2(ch, side)):
                copy.wait_send()
    for ch in range(2):
        mine[ch].wait()
        place_wait(ch)


def per_device(dlog, dener, energy, mask, owner):
    walkers, width = dlog.shape
    anywhere = pl.BlockSpec(memory_space=pl.ANY)
    dma = pltpu.SemaphoreType.DMA
    both = pl.pallas_call(
        kernel,
        out_shape=jax.ShapeDtypeStruct((2, BLOCK, width), BF16),
        in_specs=[anywhere] * 5,
        out_specs=anywhere,
        scratch_shapes=[
            pltpu.SMEM((16,), jnp.int32),
            pltpu.SMEM((16,), jnp.int32),
            pltpu.VMEM((walkers // 128, 128), F32),
            pltpu.VMEM((8, walkers, BLOCK), BF16),
            pltpu.VMEM((walkers, width), BF16),
            pltpu.VMEM((walkers, width), BF16),
            pltpu.VMEM((walkers, width), BF16),
            pltpu.VMEM((2, 2, 2, walkers, BLOCK), BF16),
            pltpu.VMEM((2 * BLOCK, walkers), BF16),
            pltpu.VMEM((walkers, 128), F32),
            pltpu.VMEM((PAIRS, 2, 2, 2, 4, 64, width), BF16),
            pltpu.VMEM((PAIRS, 2, 2, 6, 64, width), BF16),
            pltpu.VMEM((PAIRS, 2, 2, 2, 4, 16, width), BF16),
            pltpu.VMEM((PAIRS, 2, 2, 6, 16, width), BF16),
            pltpu.VMEM((2, 2, 2, 2, 4, 64, BLOCK), BF16),
            pltpu.VMEM((2, 2, 2, 6, 64, BLOCK), BF16),
            pltpu.VMEM((2, 2, 2, 2, 4, 16, BLOCK), BF16),
            pltpu.VMEM((2, 2, 2, 6, 16, BLOCK), BF16),
            pltpu.VMEM((2, 4, 2, 16, BLOCK), BF16),
            pltpu.VMEM((2, 4, 2, 16, BLOCK), BF16),
            pltpu.VMEM((16, 16, width), F32),
            pltpu.VMEM((16, 16, width), F32),
            pltpu.VMEM((8, 2, 16, width), F32),
            pltpu.VMEM((2, 16, 16, width), BF16),
            pltpu.VMEM((2, 5, 2, 8, BLOCK), F32),
            pltpu.VMEM((4, 2, 8, BLOCK), F32),
            pltpu.VMEM((2, 8, BLOCK), F32),
            dma((6,)), dma((8,)), dma((8,)), dma((2,)), dma((2,)), dma((4,)), dma((4,)), dma((4,)), dma((4,)),
            dma((ROUNDS, 2, 2, 6)), dma((ROUNDS, 2, 2, 6)), dma((ROUNDS, 2, 2, 6)), dma((ROUNDS, 2, 2, 6)),
            dma((8, 2)), dma((8, 2)), dma((16, 2)), dma((16, 2)),
            dma((2, 4)), dma((2, 4)), dma((2, 4)), dma((2, 4)),
        ],
        compiler_params=pltpu.CompilerParams(
            collective_id=0, has_side_effects=True, vmem_limit_bytes=64 * 1000 * 1000
        ),
    )(mask, owner, dlog, dener, energy.reshape(walkers // 128, 128))
    return both[0].astype(F32), both[1].astype(F32)


def solution(mesh):
    return jax.shard_map(
        per_device,
        mesh=mesh,
        in_specs=(P("walk", "pan"), P("walk", "pan"), P("walk"), P(), P()),
        out_specs=(P("walk", "pan"), P("walk", "pan")),
        check_vma=False,
    )
```

time: 117 us -> 112 us (0.957)
  Pallas kernels: 114 us -> 109 us
    pallas_call x1, Pallas kernels: 114 us -> 109 us  [per_device(): pl.pallas_call(kernel, out_shape=jax.ShapeDtypeStruct((2, BLOCK, width),...]
where the time goes in v4:
time: 112 us
  Pallas kernels  109 us (97%)
  other arithmetic  2.13 us (2%)
    pallas_call x1, Pallas kernels, per_device(): pl.pallas_call(kernel, out_shape=jax.ShapeDtypeStruct((2, BLOCK, width),...  109 us

profile of v4, /device:TPU:1, one launch (start us, length us, event | category | flops | bytes accessed | tf_op | source)
XLA Modules:
  0.0 112.0 jit_solution(3017361404783757943)
XLA Ops:
  0.6 109.2 %shard_map.68 = bf16[2,256,512]{2,1,0:T(8,128)(2,1)} custom-call(s32[16]{0:T(128)} %mask_in.1, s32[16]{0:T(128)} %owner_in.1, bf16[2048,512]{1,0:T(8,128)(2,1)} %dlog.1, bf16[2048,512]{1,0:T(8,128)(2,1)} %dener.1, f32[16,128]{1,0:T(8,128)} %bitcast.7), custom_call_target="tpu_custom_call" | custom-call | tf_op jit(solution)/shard_map/pallas_call | solution.py:461
  109.9 2.1 %bitcast_convert_fusion = (f32[256,512]{1,0:T(8,128)}, f32[256,512]{1,0:T(8,128)}) fusion(bf16[2,256,512]{2,1,0:T(8,128)(2,1)} %shard_map.68), kind=kLoop, calls=%fused_computation | loop fusion | flops 262144 | bytes 1572864 | tf_op jit(solution)/shard_map/convert_element_type | solution.py:503

commit v5 on v4

--- a/solution.py
+++ b/solution.py
@@ -375,15 +375,15 @@
 
     between = {
         1: (lambda: every(mid1, 0), None, lambda: every(fin1, 0), None),
-        2: (lambda: every(mid2, 1), None, lambda: finish_both(1), None),
+        2: (lambda: every(mid2, 1), None, None, None),
         3: (None, None, None, None),
-        4: (lambda: every(mid2, 2), lambda: every(fin1, 3), lambda: finish_both(2), None),
+        4: (None, None, None, lambda: every(fin1, 3)),
     }
     after = {
-        1: ((every, mid2, 0), (finish_both, 0), (every, mid1, 1), (every, fin1, 1)),
-        2: (),
-        3: ((every, mid1, 2), (every, fin1, 2), (every, mid1, 3)),
-        4: ((every, mid1, 4), (every, mid2, 3)),
+        1: ((every, mid1, 1), (every, mid2, 0), (every, fin1, 1), (finish_both, 0)),
+        2: ((finish_both, 1), (every, mid1, 2)),
+        3: ((every, fin1, 2), (every, mid1, 3), (every, mid2, 2)),
+        4: (),
     }
     for r in range(1, ROUNDS):
         gathered(r)
@@ -436,6 +436,10 @@
         lax.fori_loop(1, 16, step, 0)
 
     by_output = [(0, 0), (0, 1), (1, 0), (1, 1)]
+    for ch, side in by_output:
+        mid1(last, ch, side)
+    every(mid2, last - 1)
+    finish_both(last - 2)
     for ch, side in by_output:
         fin1(last, ch, side)
     finish_both(last - 1)

time: 112 us -> 108 us (0.964)
  Pallas kernels: 109 us -> 105 us
    pallas_call x1, Pallas kernels: 109 us -> 105 us  [per_device(): pl.pallas_call(kernel, out_shape=jax.ShapeDtypeStruct((2, BLOCK, width),...]
where the time goes in v5:
time: 108 us
  Pallas kernels  105 us (97%)
  other arithmetic  2.13 us (2%)
    pallas_call x1, Pallas kernels, per_device(): pl.pallas_call(kernel, out_shape=jax.ShapeDtypeStruct((2, BLOCK, width),...  105 us

profile of v5, /device:TPU:1, one launch (start us, length us, event | category | flops | bytes accessed | tf_op | source)
XLA Modules:
  0.0 108.0 jit_solution(12420268431708877556)
XLA Ops:
  0.6 105.3 %shard_map.68 = bf16[2,256,512]{2,1,0:T(8,128)(2,1)} custom-call(s32[16]{0:T(128)} %mask_in.1, s32[16]{0:T(128)} %owner_in.1, bf16[2048,512]{1,0:T(8,128)(2,1)} %dlog.1, bf16[2048,512]{1,0:T(8,128)(2,1)} %dener.1, f32[16,128]{1,0:T(8,128)} %bitcast.7), custom_call_target="tpu_custom_call" | custom-call | tf_op jit(solution)/shard_map/pallas_call | solution.py:465
  105.9 2.1 %bitcast_convert_fusion = (f32[256,512]{1,0:T(8,128)}, f32[256,512]{1,0:T(8,128)}) fusion(bf16[2,256,512]{2,1,0:T(8,128)(2,1)} %shard_map.68), kind=kLoop, calls=%fused_computation | loop fusion | flops 262144 | bytes 1572864 | tf_op jit(solution)/shard_map/convert_element_type | solution.py:507
